TPU v7x, 256 devices: a whole 4x4x8 slice. The times are simulated.
256 devices in a mesh: dp: 4 (over x), seq: 8 (over z_lo, y), tensor: 8 (over z_hi, core).
Axes of the slice: x: 4, y: 4, z: 8 (z_hi: 4, z_lo: 2; z = z_hi * 2 + z_lo), core: 2. Of those that a mesh axis runs over, the one named last changes fastest.
Arguments:
- hidden: bfloat16 [4096, 28672], P(('dp', 'seq'), 'tensor'), may hold values from -6 to 6
- weight: bfloat16 [28672, 4096], P('tensor', 'seq'), may hold values from -0.03125 to 0.03125
- out_grad: bfloat16 [4096, 4096], P(('dp', 'tensor'), 'seq'), may hold values from -6 to 6
Outputs:
- output: bfloat16 [4096, 4096], P(('dp', 'tensor'), 'seq')
- grad_hidden: bfloat16 [4096, 28672], P(('dp', 'seq'), 'tensor')
- grad_weight: bfloat16 [28672, 4096], P('tensor', 'seq')
All inputs are finite; a program needn't handle non-finite values.
Results may differ from a plain program's by a relative error of at most 0.017.
Values may be sent and summed in bfloat16 or wider, within the bound.
A program may use at most 128 MiB of HBM per device.

v0:
```python
import jax
import jax.numpy as jnp
from jax import lax
from jax.sharding import PartitionSpec as P

HB = 512


def partner_2(shard, axis, distance):
    return lax.ppermute(shard, axis, [(i, i ^ 1 << distance) for i in range(lax.axis_size(axis))])


def walsh_table(table_order):
    matrix = jnp.ones((1, 1), jnp.float32)
    while matrix.shape[0] < table_order:
        matrix = jnp.concatenate(
            [jnp.concatenate([matrix, matrix], 1), jnp.concatenate([matrix, -matrix], 1)], 0
        )
    return matrix


def local_blocks(values, inner_table):
    row_count, feature_count = values.shape
    block_size = inner_table.shape[0]
    shaped = values.reshape(row_count, feature_count // block_size, block_size)
    if values.dtype == jnp.bfloat16:
        mixed_rows = jnp.einsum(
            "rbk,kl->rbl",
            shaped,
            inner_table.astype(jnp.bfloat16),
            preferred_element_type=jnp.float32,
        )
    else:
        mixed_rows = jnp.einsum("rbk,kl->rbl", shaped, inner_table, precision=lax.Precision.HIGHEST)
    return mixed_rows.reshape(row_count, feature_count)


def butterfly(values):
    axis_count = lax.axis_size("tensor")
    device_index = lax.axis_index("tensor")
    for bit_index in range(axis_count.bit_length() - 1):
        partner = partner_2(values.astype(jnp.bfloat16), "tensor", bit_index).astype(values.dtype)
        upper_half = device_index // (1 << bit_index) % 2 == 1
        values = jnp.where(upper_half, partner - values, values + partner)
    return values


def rotate(values, inner_table, norm_scale):
    return (butterfly(local_blocks(values, inner_table)) * norm_scale).astype(jnp.bfloat16)


def body(hidden, weight, out_grad):
    inner_table = walsh_table(HB)
    norm_scale = 1.0 / float(lax.axis_size("tensor") * HB) ** 0.5
    rotated = rotate(hidden, inner_table, norm_scale)
    gathered = lax.all_gather(rotated, "seq", axis=0, tiled=True)
    partial_sums = jnp.dot(gathered, weight, preferred_element_type=jnp.float32)
    output = lax.psum_scatter(
        partial_sums.astype(jnp.bfloat16), "tensor", scatter_dimension=0, tiled=True
    )
    grads_all = lax.all_gather(out_grad, "tensor", axis=0, tiled=True)
    token_total = hidden.shape[0] * lax.axis_size("seq") * lax.axis_size("dp")
    grad_term = lax.dot_general(
        gathered, grads_all, (((0,), (0,)), ((), ())), preferred_element_type=jnp.float32
    )
    grad_weight = lax.psum(
        (grad_term * (1.0 / float(token_total) ** 0.5)).astype(jnp.bfloat16), "dp"
    )
    rotated_grad = lax.psum_scatter(
        lax.dot_general(
            grads_all, weight, (((1,), (1,)), ((), ())), preferred_element_type=jnp.float32
        ).astype(jnp.bfloat16),
        "seq",
        scatter_dimension=0,
        tiled=True,
    ).astype(jnp.float32)
    grad_hidden = rotate(rotated_grad, inner_table, norm_scale)
    return (output, grad_hidden, grad_weight)


def solution(mesh):
    in_specs = (P(("dp", "seq"), "tensor"), P("tensor", "seq"), P(("dp", "tensor"), "seq"))
    out_specs = (P(("dp", "tensor"), "seq"), P(("dp", "seq"), "tensor"), P("tensor", "seq"))
    return jax.shard_map(body, mesh=mesh, in_specs=in_specs, out_specs=out_specs, check_vma=False)
```

profile of v0, /device:TPU:1, one launch (start us, length us, event | category | flops | bytes accessed | tf_op | source)
XLA Modules:
  0.0 447.1 jit_solution(14021014759159372248)
XLA Ops:
  7.2 0.7 all-gather.5.cloned.1.call-update
  7.9 36.3 %all-gather.5.cloned.1.call-done = bf16[1024,512]{1,0:T(8,128)(2,1)} async-done(((bf16[128,512]{1,0:T(8,128)(2,1)}), bf16[1024,512]{1,0:T(8,128)(2,1)}) %all-gather.5.cloned.1.call-update) | async-done | bytes 1048592 | tf_op jit(solution)/shard_map/all_gather | solution.py:61
  44.2 9.3 %convolution_convert_fusion = bf16[1024,3584]{1,0:T(8,128)(2,1)} fusion(bf16[1024,512]{1,0:T(8,128)(2,1)} %all-gather.5.cloned.1.call-done, bf16[3584,512]{1,0:T(8,128)(2,1)} %param.4), kind=kOutput, calls=%fused_computation | convolution fusion | flops 3761766400 | bytes 12058624 | tf_op jit(solution)/shard_map/dot_general | solution.py:70
  53.6 1.1 copy-done
  54.7 0.6 copy.11
  55.3 0.7 fusion.14
  56.0 1.0 bitcast_convert_fusion.1
  57.4 2.4 collective-permute-done
  59.7 1.2 fusion.13
  61.0 1.6 collective-permute-start.1
  62.5 41.3 %collective-permute-done.1 = bf16[128,3584]{0,1:T(8,128)(2,1)} collective-permute-done((bf16[128,3584]{0,1:T(8,128)(2,1)}, bf16[128,3584]{0,1:T(8,128)(2,1)}, u32[]{:S(2)}, u32[]{:S(2)}) %collective-permute-start.1) | collective-permute-done | bytes 917536 | tf_op jit(solution)/shard_map/ppermute | solution.py:10
  103.8 2.6 fusion.11
  106.5 2.7 collective-permute-start.2
  109.2 62.5 %collective-permute-done.2 = bf16[128,3584]{0,1:T(8,128)(2,1)} collective-permute-done((bf16[128,3584]{0,1:T(8,128)(2,1)}, bf16[128,3584]{0,1:T(8,128)(2,1)}, u32[]{:S(2)}, u32[]{:S(2)}) %collective-permute-start.2) | collective-permute-done | bytes 917536 | tf_op jit(solution)/shard_map/ppermute | solution.py:10
  171.7 3.2 fusion.4
  175.0 20.5 %reduce-scatter.5.cloned.1.call-done = bf16[128,3584]{1,0:T(8,128)(2,1)} async-done(((bf16[1024,3584]{1,0:T(8,128)(2,1)}), bf16[128,3584]{1,0:T(8,128)(2,1)}) %reduce-scatter.5.cloned.1.call-update) | async-done | bytes 917520 | tf_op jit(solution)/shard_map/reduce_scatter | solution.py:69
  195.5 1.5 copy.13
  197.0 3.1 fusion.15
  200.1 1.0 bitcast_convert_fusion
  201.5 79.5 %all-gather.3.cloned.1.call-done = bf16[1024,3584]{0,1:T(8,128)(2,1)} async-done(((bf16[128,3584]{0,1:T(8,128)(2,1)}), bf16[1024,3584]{0,1:T(8,128)(2,1)}) %all-gather.3.cloned.1.call-update) | async-done | bytes 7340048 | tf_op jit(solution)/shard_map/all_gather | solution.py:56
  281.0 9.1 %convolution_convert_fusion.1 = bf16[1024,512]{1,0:T(8,128)(2,1)} fusion(bf16[1024,3584]{0,1:T(8,128)(2,1)} %all-gather.3.cloned.1.call-done, bf16[3584,512]{1,0:T(8,128)(2,1)} %param.4), kind=kOutput, calls=%fused_computation.26 | convolution fusion | flops 3758620672 | bytes 12058624 | tf_op jit(solution)/shard_map/dot_general | solution.py:57
  290.2 1.2 fusion.12
  291.4 2.3 collective-permute-start.4
  293.7 8.5 %multiply_convert_fusion = bf16[3584,512]{1,0:T(8,128)(2,1)} fusion(bf16[1024,3584]{0,1:T(8,128)(2,1)} %all-gather.3.cloned.1.call-done, bf16[1024,512]{1,0:T(8,128)(2,1)S(1)} %copy-done.2), kind=kOutput, calls=%fused_computation.1 | convolution fusion | flops 3761766400 | bytes 12058624 | tf_op jit(solution)/shard_map/dot_general | solution.py:63
  302.2 41.2 %collective-permute-done.4 = bf16[128,3584]{0,1:T(8,128)(2,1)} collective-permute-done((bf16[128,3584]{0,1:T(8,128)(2,1)}, bf16[128,3584]{0,1:T(8,128)(2,1)}, u32[]{:S(2)}, u32[]{:S(2)}) %collective-permute-start.4) | collective-permute-done | bytes 917536 | tf_op jit(solution)/shard_map/ppermute | solution.py:10
  343.4 1.7 fusion.10
  345.1 6.5 %collective-permute-start.5 = (bf16[128,3584]{0,1:T(8,128)(2,1)S(1)}, bf16[128,3584]{0,1:T(8,128)(2,1)S(1)}, u32[]{:S(2)}, u32[]{:S(2)}) collective-permute-start(bf16[128,3584]{0,1:T(8,128)(2,1)S(1)} %fusion.10), channel_id=1, source_target_pairs={{0,4},{1,5},{2,6},{3,7},{4,0},{5,1},{6,2},{7,3},{8,12},{9,13},{10,... | collective-permute-start | bytes 2752520 | tf_op jit(solution)/shard_map/ppermute | solution.py:10
  351.6 40.0 %collective-permute-done.5 = bf16[128,3584]{0,1:T(8,128)(2,1)S(1)} collective-permute-done((bf16[128,3584]{0,1:T(8,128)(2,1)S(1)}, bf16[128,3584]{0,1:T(8,128)(2,1)S(1)}, u32[]{:S(2)}, u32[]{:S(2)}) %collective-permute-start.5) | collective-permute-done | bytes 917536 | tf_op jit(solution)/shard_map/ppermute | solution.py:10
  391.6 3.0 fusion.9
  394.6 2.2 copy.16
  396.8 39.6 %all-reduce.2.cloned.1.call-done = bf16[3584,512]{1,0:T(8,128)(2,1)} async-done(((bf16[3584,512]{1,0:T(8,128)(2,1)}), bf16[3584,512]{1,0:T(8,128)(2,1)}) %all-reduce.2.cloned.1.call-update) | async-done | bytes 3670032 | tf_op jit(solution)/shard_map/psum | solution.py:66
  436.4 4.1 copy.21
  (18 shorter events, 1.0 us)
Async XLA Ops:
  7.2 37.1 %all-gather.5.cloned.1.call-start = ((), (), s32[]{:S(2)}) async-start(), calls=%async_computation.4 | async-start | bytes 1179648 | tf_op jit(solution)/shard_map/all_gather | solution.py:61
  7.9 187.6 %reduce-scatter.5.cloned.1.call-start = ((), (), s32[]{:S(2)}) async-start(), calls=%async_computation.5 | async-start | bytes 8257536 | tf_op jit(solution)/shard_map/reduce_scatter | solution.py:69
  53.5 1.2 copy-start
  53.6 1.8 copy-start.1
  53.6 227.5 %all-gather.3.cloned.1.call-start = ((), (), s32[]{:S(2)}) async-start(), calls=%async_computation.2 | async-start | bytes 8257536 | tf_op jit(solution)/shard_map/all_gather | solution.py:56
  57.1 2.7 collective-permute-start
  61.0 42.9 %collective-permute-start.1 = (bf16[128,3584]{0,1:T(8,128)(2,1)}, bf16[128,3584]{0,1:T(8,128)(2,1)}, u32[]{:S(2)}, u32[]{:S(2)}) collective-permute-start(bf16[128,3584]{0,1:T(8,128)(2,1)} %fusion.13), channel_id=1, source_target_pairs={{0,2},{1,3},{2,0},{3,1},{4,6},{5,7},{6,4},{7,5},{8,10},{9,11},{10,... | collective-permute-start | bytes 2752520 | tf_op jit(solution)/shard_map/ppermute | solution.py:10
  106.5 65.2 %collective-permute-start.2 = (bf16[128,3584]{0,1:T(8,128)(2,1)}, bf16[128,3584]{0,1:T(8,128)(2,1)}, u32[]{:S(2)}, u32[]{:S(2)}) collective-permute-start(bf16[128,3584]{0,1:T(8,128)(2,1)} %fusion.11), channel_id=1, source_target_pairs={{0,4},{1,5},{2,6},{3,7},{4,0},{5,1},{6,2},{7,3},{8,12},{9,13},{10,... | collective-permute-start | bytes 2752520 | tf_op jit(solution)/shard_map/ppermute | solution.py:10
  175.0 221.8 %reduce-scatter.3.cloned.1.call-start = ((), (), s32[]{:S(2)}) async-start(), calls=%async_computation.3 | async-start | bytes 1179648 | tf_op jit(solution)/shard_map/reduce_scatter | solution.py:58
  201.1 89.1 %collective-permute-start.3 = (bf16[128,3584]{0,1:T(8,128)(2,1)}, bf16[128,3584]{0,1:T(8,128)(2,1)S(1)}, u32[]{:S(2)}, u32[]{:S(2)}) collective-permute-start(bf16[128,3584]{0,1:T(8,128)(2,1)} %bitcast_convert_fusion), channel_id=1, source_target_pairs={{0,1},{1,0},{2,3},{3,2},{4,5},{5,4},{6,7},{7,6},{8,9},{9,8},{10,11... | collective-permute-start | bytes 2752520 | tf_op jit(solution)/shard_map/ppermute | solution.py:10
  290.1 146.3 %all-reduce.2.cloned.1.call-start = ((), (), s32[]{:S(2)}) async-start(), calls=%async_computation.6 | async-start | bytes 7340032 | tf_op jit(solution)/shard_map/psum | solution.py:66
  290.2 3.5 copy-start.2
  291.4 52.0 %collective-permute-start.4 = (bf16[128,3584]{0,1:T(8,128)(2,1)}, bf16[128,3584]{0,1:T(8,128)(2,1)}, u32[]{:S(2)}, u32[]{:S(2)}) collective-permute-start(bf16[128,3584]{0,1:T(8,128)(2,1)} %fusion.12), channel_id=1, source_target_pairs={{0,2},{1,3},{2,0},{3,1},{4,6},{5,7},{6,4},{7,5},{8,10},{9,11},{10,... | collective-permute-start | bytes 2752520 | tf_op jit(solution)/shard_map/ppermute | solution.py:10
  345.1 46.4 %collective-permute-start.5 = (bf16[128,3584]{0,1:T(8,128)(2,1)S(1)}, bf16[128,3584]{0,1:T(8,128)(2,1)S(1)}, u32[]{:S(2)}, u32[]{:S(2)}) collective-permute-start(bf16[128,3584]{0,1:T(8,128)(2,1)S(1)} %fusion.10), channel_id=1, source_target_pairs={{0,4},{1,5},{2,6},{3,7},{4,0},{5,1},{6,2},{7,3},{8,12},{9,13},{10,... | collective-permute-start | bytes 2752520 | tf_op jit(solution)/shard_map/ppermute | solution.py:10
Sparse Core Ops, SparseCore 0:
  9.8 34.3 all-gather.4
  53.7 141.7 reduce-scatter.4
  197.8 83.2 all-gather.2
  290.3 50.2 reduce-scatter.2
  343.4 93.0 all-reduce.1
where the time goes:
time: 447 us
  waiting for transfers between devices  364 us (81%)
  matrix products  30.6 us (7%)
  other arithmetic  15 us (3%)
  starting transfers between devices  13.9 us (3%)
  between operations  13.8 us (3%)
  local copies, waits for them, and re-layouts  9.58 us (2%)
    ppermute x6, waiting for transfers between devices, partner_2(): lax.ppermute(shard, axis, [(i, i ^ 1 << distance) for i in range(lax.axis...  187 us
    all_gather x1, waiting for transfers between devices, body(): gathered = lax.all_gather(rotated, 'seq', axis=0, tiled=True)  79.5 us
    psum x1, waiting for transfers between devices, body(): lax.psum((grad_term * (1.0 / float(token_total) ** 0.5)).astype(jnp.bfloa...  39.6 us
    all_gather x1, waiting for transfers between devices, body(): grads_all = lax.all_gather(out_grad, 'tensor', axis=0, tiled=True)  36.3 us
    reduce_scatter x1, waiting for transfers between devices, body(): lax.psum_scatter(lax.dot_general(grads_all, weight, (((1,), (1,)), ((), (...  20.5 us
    ppermute x6, starting transfers between devices, partner_2(): lax.ppermute(shard, axis, [(i, i ^ 1 << distance) for i in range(lax.axis...  13.7 us
    dot_general x1, matrix products, body(): lax.dot_general(grads_all, weight, (((1,), (1,)), ((), ())), preferred_el...  9.3 us
    dot_general x1, matrix products, body(): partial_sums = jnp.dot(gathered, weight, preferred_element_type=jnp.float32)  9.08 us
  transfers between devices with their start and end apart: 11, of which 9 were waited for; matrix products, arithmetic and copies ran while one was open for 9% of the time, Pallas kernels for 0%

commit v1 on v0

--- a/solution.py
+++ b/solution.py
@@ -63,8 +63,9 @@
     grad_term = lax.dot_general(
         gathered, grads_all, (((0,), (0,)), ((), ())), preferred_element_type=jnp.float32
     )
-    grad_weight = lax.psum(
-        (grad_term * (1.0 / float(token_total) ** 0.5)).astype(jnp.bfloat16), "dp"
+    build_the_cells = lambda sample: jax.lax.all_gather(sample, axis_name="dp").sum(axis=0)
+    grad_weight = build_the_cells(
+        (grad_term * (1.0 / float(token_total) ** 0.5)).astype(jnp.bfloat16)
     )
     rotated_grad = lax.psum_scatter(
         lax.dot_general(

time: 447 us -> 490 us (1.096)
  waiting for transfers between devices: 364 us -> 398 us
  other arithmetic: 15 us -> 24.8 us
    reduce_scatter x1, waiting for transfers between devices: 20.5 us -> 82.5 us  [body(): lax.psum_scatter(lax.dot_general(grads_all, weight, (((1,), (1,)), ((), (...]
    psum x1 -> x0, waiting for transfers between devices: 39.6 us -> none  [body(): lax.psum((grad_term * (1.0 / float(token_total) ** 0.5)).astype(jnp.bfloa...]
    all_gather x0 -> x1, waiting for transfers between devices: none -> 35.7 us  [body(): jax.lax.all_gather(sample, axis_name='dp').sum(axis=0)]
    reduce_scatter x1, waiting for transfers between devices: 0.01 us -> 31.2 us  [body(): lax.psum_scatter(partial_sums.astype(jnp.bfloat16), 'tensor', scatter_dim...]
    all_gather x1, waiting for transfers between devices: 36.3 us -> 6.73 us  [body(): grads_all = lax.all_gather(out_grad, 'tensor', axis=0, tiled=True)]
    ppermute x6, waiting for transfers between devices: 187 us -> 164 us  [partner_2(): lax.ppermute(shard, axis, [(i, i ^ 1 << distance) for i in range(lax.axis...]
    reduce_sum x0 -> x1, other arithmetic: none -> 10.7 us  [body(): jax.lax.all_gather(sample, axis_name='dp').sum(axis=0)]
  transfers between devices with their start and end apart: 11 -> 11, of which waited for: 9 -> 11; matrix products, arithmetic and copies ran while one was open for 9% -> 11% of each run, Pallas kernels for 0% -> 0%
where the time goes in v1:
time: 490 us; the launch traced here: 488 us
  waiting for transfers between devices  398 us (81%)
  matrix products  29.4 us (6%)
  other arithmetic  24.8 us (5%)
  starting transfers between devices  17 us (3%)
  between operations  13.9 us (3%)
  local copies, waits for them, and re-layouts  5.39 us (1%)
    ppermute x6, waiting for transfers between devices, partner_2(): lax.ppermute(shard, axis, [(i, i ^ 1 << distance) for i in range(lax.axis...  164 us
    reduce_scatter x1, waiting for transfers between devices, body(): lax.psum_scatter(lax.dot_general(grads_all, weight, (((1,), (1,)), ((), (...  82.5 us
    all_gather x1, waiting for transfers between devices, body(): gathered = lax.all_gather(rotated, 'seq', axis=0, tiled=True)  77.5 us
    all_gather x1, waiting for transfers between devices, body(): jax.lax.all_gather(sample, axis_name='dp').sum(axis=0)  35.7 us
    reduce_scatter x1, waiting for transfers between devices, body(): lax.psum_scatter(partial_sums.astype(jnp.bfloat16), 'tensor', scatter_dim...  31.2 us
    ppermute x6, starting transfers between devices, partner_2(): lax.ppermute(shard, axis, [(i, i ^ 1 << distance) for i in range(lax.axis...  16.6 us
    reduce_sum x1, other arithmetic, body(): jax.lax.all_gather(sample, axis_name='dp').sum(axis=0)  10.7 us
  transfers between devices with their start and end apart: 11, of which 11 were waited for; matrix products, arithmetic and copies ran while one was open for 11% of the time, Pallas kernels for 0%

profile of v1, /device:TPU:1, one launch (start us, length us, event | category | flops | bytes accessed | tf_op | source)
XLA Modules:
  0.0 488.3 jit_solution(17500396318208574208)
XLA Ops:
  7.2 1.6 copy.11
  9.6 1.0 bitcast_convert_fusion.1
  10.6 3.2 collective-permute-start
  13.8 2.3 collective-permute-done
  16.1 1.2 fusion.13
  17.3 1.3 collective-permute-start.1
  18.6 41.6 %collective-permute-done.1 = bf16[128,3584]{0,1:T(8,128)(2,1)} collective-permute-done((bf16[128,3584]{0,1:T(8,128)(2,1)}, bf16[128,3584]{0,1:T(8,128)(2,1)}, u32[]{:S(2)}, u32[]{:S(2)}) %collective-permute-start.1) | collective-permute-done | bytes 917536 | tf_op jit(solution)/shard_map/ppermute | solution.py:10
  60.2 2.6 fusion.11
  62.8 5.0 %collective-permute-start.2 = (bf16[128,3584]{0,1:T(8,128)(2,1)}, bf16[128,3584]{0,1:T(8,128)(2,1)}, u32[]{:S(2)}, u32[]{:S(2)}) collective-permute-start(bf16[128,3584]{0,1:T(8,128)(2,1)} %fusion.11), channel_id=1, source_target_pairs={{0,4},{1,5},{2,6},{3,7},{4,0},{5,1},{6,2},{7,3},{8,12},{9,13},{10,... | collective-permute-start | bytes 2752520 | tf_op jit(solution)/shard_map/ppermute | solution.py:10
  67.9 44.0 %collective-permute-done.2 = bf16[128,3584]{0,1:T(8,128)(2,1)} collective-permute-done((bf16[128,3584]{0,1:T(8,128)(2,1)}, bf16[128,3584]{0,1:T(8,128)(2,1)}, u32[]{:S(2)}, u32[]{:S(2)}) %collective-permute-start.2) | collective-permute-done | bytes 917536 | tf_op jit(solution)/shard_map/ppermute | solution.py:10
  112.0 3.2 fusion.4
  115.3 6.7 %all-gather.7.cloned.1.call-done = bf16[1024,512]{1,0:T(8,128)(2,1)} async-done(((bf16[128,512]{1,0:T(8,128)(2,1)}), bf16[1024,512]{1,0:T(8,128)(2,1)}) %all-gather.7.cloned.1.call-update) | async-done | bytes 1048592 | tf_op jit(solution)/shard_map/all_gather | solution.py:61
  122.0 9.3 %convolution_convert_fusion = bf16[1024,3584]{1,0:T(8,128)(2,1)} fusion(bf16[1024,512]{1,0:T(8,128)(2,1)} %all-gather.7.cloned.1.call-done, bf16[3584,512]{1,0:T(8,128)(2,1)} %param.4), kind=kOutput, calls=%fused_computation | convolution fusion | flops 3761766400 | bytes 12058624 | tf_op jit(solution)/shard_map/dot_general | solution.py:71
  131.4 77.5 %all-gather.5.cloned.1.call-done = bf16[1024,3584]{0,1:T(8,128)(2,1)} async-done(((bf16[128,3584]{0,1:T(8,128)(2,1)}), bf16[1024,3584]{0,1:T(8,128)(2,1)}) %all-gather.5.cloned.1.call-update) | async-done | bytes 7340048 | tf_op jit(solution)/shard_map/all_gather | solution.py:56
  208.9 8.5 %multiply_convert_fusion = bf16[3584,512]{1,0:T(8,128)(2,1)} fusion(bf16[1024,3584]{0,1:T(8,128)(2,1)} %all-gather.5.cloned.1.call-done, bf16[1024,512]{1,0:T(8,128)(2,1)S(1)} %copy-done.2), kind=kOutput, calls=%fused_computation.1 | convolution fusion | flops 3761766400 | bytes 12058624 | tf_op jit(solution)/shard_map/dot_general | solution.py:63
  217.6 82.5 %reduce-scatter.5.cloned.1.call-done = bf16[128,3584]{1,0:T(8,128)(2,1)} async-done(((bf16[1024,3584]{1,0:T(8,128)(2,1)}), bf16[128,3584]{1,0:T(8,128)(2,1)}) %reduce-scatter.5.cloned.1.call-update) | async-done | bytes 917520 | tf_op jit(solution)/shard_map/reduce_scatter | solution.py:70
  300.1 1.5 copy.13
  301.6 3.1 fusion.15
  304.8 0.8 collective-permute-start.3
  305.6 2.1 collective-permute-done.3
  307.7 1.2 fusion.12
  308.9 2.3 collective-permute-start.4
  311.2 7.9 %convolution_convert_fusion.1 = bf16[1024,512]{1,0:T(8,128)(2,1)} fusion(bf16[1024,3584]{0,1:T(8,128)(2,1)} %all-gather.5.cloned.1.call-done, bf16[3584,512]{1,0:T(8,128)(2,1)S(1)} %copy-done.1), kind=kOutput, calls=%fused_computation.26 | convolution fusion | flops 3758620672 | bytes 12058624 | tf_op jit(solution)/shard_map/dot_general | solution.py:57
  319.1 32.9 %collective-permute-done.4 = bf16[128,3584]{0,1:T(8,128)(2,1)} collective-permute-done((bf16[128,3584]{0,1:T(8,128)(2,1)}, bf16[128,3584]{0,1:T(8,128)(2,1)}, u32[]{:S(2)}, u32[]{:S(2)}) %collective-permute-start.4) | collective-permute-done | bytes 917536 | tf_op jit(solution)/shard_map/ppermute | solution.py:10
  352.0 1.7 fusion.10
  353.7 4.0 collective-permute-start.5
  357.7 41.2 %collective-permute-done.5 = bf16[128,3584]{0,1:T(8,128)(2,1)S(1)} collective-permute-done((bf16[128,3584]{0,1:T(8,128)(2,1)S(1)}, bf16[128,3584]{0,1:T(8,128)(2,1)S(1)}, u32[]{:S(2)}, u32[]{:S(2)}) %collective-permute-start.5) | collective-permute-done | bytes 917536 | tf_op jit(solution)/shard_map/ppermute | solution.py:10
  398.9 3.0 fusion.9
  401.9 2.2 copy.16
  404.1 35.7 %all-gather.9.cloned.1.call-done = bf16[14336,512]{1,0:T(8,128)(2,1)} async-done(((bf16[3584,512]{1,0:T(8,128)(2,1)}), bf16[14336,512]{1,0:T(8,128)(2,1)}) %all-gather.9.cloned.1.call-update) | async-done | bytes 14680080 | tf_op jit(solution)/shard_map/all_gather | solution.py:66
  439.8 10.7 %reduce_sum.12 = bf16[3584,512]{1,0:T(8,128)(2,1)} reduce(bf16[4,3584,512]{2,1,0:T(8,128)(2,1)} %bitcast.35, bf16[]{:T(256)} %constant.80.clone.1), dimensions={0}, to_apply=%region_2.3 | reduce | flops 5505024 | bytes 18350082 | tf_op jit(solution)/shard_map/reduce_sum | solution.py:66
  450.5 31.2 %reduce-scatter.3.cloned.1.call-done = bf16[128,512]{1,0:T(8,128)(2,1)} async-done(((bf16[1024,512]{1,0:T(8,128)(2,1)}), bf16[128,512]{1,0:T(8,128)(2,1)}) %reduce-scatter.3.cloned.1.call-update) | async-done | bytes 131088 | tf_op jit(solution)/shard_map/reduce_scatter | solution.py:58
  (18 shorter events, 1.3 us)
Async XLA Ops:
  7.2 1.7 copy-start
  7.2 114.8 %all-gather.7.cloned.1.call-start = ((), (), s32[]{:S(2)}) async-start(), calls=%async_computation.4 | async-start | bytes 1179648 | tf_op jit(solution)/shard_map/all_gather | solution.py:61
  10.6 5.5 %collective-permute-start = (bf16[128,3584]{0,1:T(8,128)(2,1)}, bf16[128,3584]{0,1:T(8,128)(2,1)S(1)}, u32[]{:S(2)}, u32[]{:S(2)}) collective-permute-start(bf16[128,3584]{0,1:T(8,128)(2,1)} %bitcast_convert_fusion.1), channel_id=1, source_target_pairs={{0,1},{1,0},{2,3},{3,2},{4,5},{5,4},{6,7},{7,6},{8,9},{9,8},{10,11... | collective-permute-start | bytes 2752520 | tf_op jit(solution)/shard_map/ppermute | solution.py:10
  17.3 42.9 %collective-permute-start.1 = (bf16[128,3584]{0,1:T(8,128)(2,1)}, bf16[128,3584]{0,1:T(8,128)(2,1)}, u32[]{:S(2)}, u32[]{:S(2)}) collective-permute-start(bf16[128,3584]{0,1:T(8,128)(2,1)} %fusion.13), channel_id=1, source_target_pairs={{0,2},{1,3},{2,0},{3,1},{4,6},{5,7},{6,4},{7,5},{8,10},{9,11},{10,... | collective-permute-start | bytes 2752520 | tf_op jit(solution)/shard_map/ppermute | solution.py:10
  62.8 49.2 %collective-permute-start.2 = (bf16[128,3584]{0,1:T(8,128)(2,1)}, bf16[128,3584]{0,1:T(8,128)(2,1)}, u32[]{:S(2)}, u32[]{:S(2)}) collective-permute-start(bf16[128,3584]{0,1:T(8,128)(2,1)} %fusion.11), channel_id=1, source_target_pairs={{0,4},{1,5},{2,6},{3,7},{4,0},{5,1},{6,2},{7,3},{8,12},{9,13},{10,... | collective-permute-start | bytes 2752520 | tf_op jit(solution)/shard_map/ppermute | solution.py:10
  67.9 141.0 %all-gather.5.cloned.1.call-start = ((), (), s32[]{:S(2)}) async-start(), calls=%async_computation.2 | async-start | bytes 8257536 | tf_op jit(solution)/shard_map/all_gather | solution.py:56
  115.2 184.9 %reduce-scatter.5.cloned.1.call-start = ((), (), s32[]{:S(2)}) async-start(), calls=%async_computation.5 | async-start | bytes 8257536 | tf_op jit(solution)/shard_map/reduce_scatter | solution.py:70
  131.3 77.5 %copy-start.2 = (bf16[1024,512]{1,0:T(8,128)(2,1)S(1)}, bf16[1024,512]{1,0:T(8,128)(2,1)}, u32[]{:S(2)}) copy-start(bf16[1024,512]{1,0:T(8,128)(2,1)} %all-gather.7.cloned.1.call-done) | copy-start | bytes 3145732
  131.3 308.5 %all-gather.9.cloned.1.call-start = ((), (), s32[]{:S(2)}) async-start(), calls=%async_computation.6 | async-start | bytes 18350080 | tf_op jit(solution)/shard_map/all_gather | solution.py:66
  217.4 264.4 %reduce-scatter.3.cloned.1.call-start = ((), (), s32[]{:S(2)}) async-start(), calls=%async_computation.3 | async-start | bytes 1179648 | tf_op jit(solution)/shard_map/reduce_scatter | solution.py:58
  304.8 6.4 %copy-start.1 = (bf16[3584,512]{1,0:T(8,128)(2,1)S(1)}, bf16[3584,512]{1,0:T(8,128)(2,1)}, u32[]{:S(2)}) copy-start(bf16[3584,512]{1,0:T(8,128)(2,1)} %param.4) | copy-start | bytes 11010052
  304.8 2.9 collective-permute-start.3
  308.9 43.1 %collective-permute-start.4 = (bf16[128,3584]{0,1:T(8,128)(2,1)}, bf16[128,3584]{0,1:T(8,128)(2,1)}, u32[]{:S(2)}, u32[]{:S(2)}) collective-permute-start(bf16[128,3584]{0,1:T(8,128)(2,1)} %fusion.12), channel_id=1, source_target_pairs={{0,2},{1,3},{2,0},{3,1},{4,6},{5,7},{6,4},{7,5},{8,10},{9,11},{10,... | collective-permute-start | bytes 2752520 | tf_op jit(solution)/shard_map/ppermute | solution.py:10
  353.7 45.2 %collective-permute-start.5 = (bf16[128,3584]{0,1:T(8,128)(2,1)S(1)}, bf16[128,3584]{0,1:T(8,128)(2,1)S(1)}, u32[]{:S(2)}, u32[]{:S(2)}) collective-permute-start(bf16[128,3584]{0,1:T(8,128)(2,1)S(1)} %fusion.10), channel_id=1, source_target_pairs={{0,4},{1,5},{2,6},{3,7},{4,0},{5,1},{6,2},{7,3},{8,12},{9,13},{10,... | collective-permute-start | bytes 2752520 | tf_op jit(solution)/shard_map/ppermute | solution.py:10
Sparse Core Ops, SparseCore 0:
  68.0 53.9 all-gather.6
  124.3 84.5 all-gather.4
  211.4 88.6 reduce-scatter.4
  302.3 137.4 all-gather.8
  442.8 38.9 reduce-scatter.2
